TPU v7x, 32 devices: a whole 2x2x4 slice. The times are simulated.
32 devices in a mesh: sample: 2 (over y), region: 4 (over x, core), sub: 4 (over z).
Axes of the slice: x: 2, y: 2, z: 4, core: 2. Of those that a mesh axis runs over, the one named last changes fastest.
Arguments:
- densities: bfloat16 [4096, 128], P(('sample', 'region', 'sub')), parts along dimension 0, may hold values from -6 to 6
- cluster_size: int32 [32], P('sample'), parts along dimension 0, may hold values from 1 to 128, 1365 in all
- near_block: bfloat16 [4096, 512], P(('sample', 'region', 'sub')), parts along dimension 0, may hold values from -0.25 to 0.25
- row_factor: bfloat16 [4096, 512], P(('sample', 'region', 'sub')), parts along dimension 0, may hold values from -0.375 to 0.375
- column_factor: bfloat16 [512, 4096], P(None, ('sample', 'region', 'sub')), parts along dimension 1, may hold values from -0.5 to 0.5
Outputs:
- applied: float32 [4096, 128], P(('sample', 'region', 'sub')), parts along dimension 0
There are 2 independent parts, one for each index of `sample`. A program takes and returns all parts, laid end to end along the dimension named above; each array names one. Nothing has to cross between parts.
Inputs may be any that keep to these rules, and one draw needn't show every extreme that they name: `cluster_size`: sizes of the 16 clusters, summing to 1365, with some cluster of exactly 128.
All inputs are finite; a program needn't handle non-finite values.
Results may differ from a plain program's by a relative error of at most 0.0022.
Values may be sent and summed in bfloat16 or wider, within the bound.
No kernel may reach another device: no remote copies, remote signals or barrier semaphores. Data moves between devices by JAX's collectives and lax.ppermute only.
A program may use at most 64 MiB of HBM per device.

v0:
```python
import jax
import jax.numpy as jnp
from jax import lax
from jax.sharding import PartitionSpec as P


def send_coefficients(coefficients):
    return lax.all_to_all(coefficients, ("region", "sub"), split_axis=0, concat_axis=0, tiled=True)


def local(densities, cluster_size, near_block, row_factor, column_factor):
    row_count, load_count = densities.shape
    group_count = lax.axis_size("sub")
    region_count = lax.axis_size("region")
    cluster_count = group_count * region_count
    rank_width = row_factor.shape[1] // cluster_count
    region_id = lax.axis_index("region")
    own_cluster = region_id * group_count + lax.axis_index("sub")
    slot_index = lax.broadcasted_iota(jnp.int32, (row_count, 1), 0)
    own_live = slot_index < cluster_size[own_cluster]
    masked = jnp.where(own_live, densities, jnp.zeros_like(densities))
    near_sum = jnp.dot(
        near_block,
        lax.all_gather(masked, "sub", axis=0, tiled=True),
        preferred_element_type=jnp.float32,
    )
    cluster_ids = jnp.arange(cluster_count, dtype=jnp.int32)
    far_flags = cluster_ids // group_count != region_id
    coefficients = jnp.dot(column_factor, masked, preferred_element_type=jnp.float32).astype(
        jnp.bfloat16
    )
    received = send_coefficients(coefficients)
    rank_flags = jnp.repeat(far_flags, rank_width)[:, None]
    received = jnp.where(rank_flags, received, jnp.zeros_like(received))
    far_sum = jnp.dot(row_factor, received, preferred_element_type=jnp.float32)
    combined = near_sum + far_sum
    return jnp.where(own_live, combined, jnp.zeros_like(combined))


def solution(mesh):
    return jax.shard_map(
        local,
        mesh=mesh,
        in_specs=(
            P(("sample", "region", "sub"), None),
            P("sample"),
            P(("sample", "region", "sub"), None),
            P(("sample", "region", "sub"), None),
            P(None, ("sample", "region", "sub")),
        ),
        out_specs=P(("sample", "region", "sub"), None),
        check_vma=False,
    )
```

profile of v0, /device:TPU:0, one launch (start us, length us, event | category | flops | bytes accessed | tf_op | source)
XLA Modules:
  0.0 28.1 jit_solution(1108674390602110613)
XLA Ops:
  0.0 0.0 copy-start
  0.0 0.0 copy-start.3
  0.0 0.7 %copy-done.3 = s32[16]{0:T(128)S(1)} copy-done((s32[16]{0:T(128)S(1)}, s32[16]{0:T(128)}, u32[]{:S(2)}) %copy-start.3) | copy-done | bytes 88
  0.7 0.6 %dynamic_slice.3 = s32[1]{0:T(128)} dynamic-slice(s32[16]{0:T(128)S(1)} %copy-done.3, s32[]{:T(128)S(6)} %select_n.23), dynamic_slice_sizes={1} | dynamic-slice | bytes 12 | tf_op jit(solution)/shard_map/dynamic_slice | solution.py:20
  1.3 0.6 %iota_compare_fusion = pred[128]{0:T(512)(128)(4,1)S(1)} fusion(s32[]{:T(128)} %bitcast), kind=kLoop, calls=%fused_computation.12 | loop fusion | flops 128 | bytes 132 | tf_op jit(solution)/shard_map/lt | solution.py:20
  1.9 0.8 %broadcast_select_fusion = bf16[128,128]{1,0:T(8,128)(2,1)S(1)} fusion(bf16[128,128]{1,0:T(8,128)(2,1)} %param.5, pred[128]{0:T(512)(128)(4,1)S(1)} %iota_compare_fusion), kind=kLoop, calls=%fused_computation.6 | loop fusion | flops 16384 | bytes 65664 | tf_op jit(solution)/shard_map/jit(_where)/select_n | solution.py:21
  2.8 0.0 copy-done
  2.8 0.2 fusion
  3.0 0.7 %copy.7 = bf16[512,128]{1,0:T(8,128)(2,1)} copy(bf16[512,128]{0,1:T(8,128)(2,1)S(1)} %fusion) | data formatting | bytes 262144 | tf_op jit(solution)/shard_map/convert_element_type | solution.py:29
  3.8 7.4 %all-to-all-start = ((bf16[16,32,128]{2,1,0:T(8,128)(2,1)}), bf16[16,32,128]{2,1,0:T(8,128)(2,1)S(1)}, u32[]{:S(2)}, u32[]{:S(2)}) async-start(bf16[16,32,128]{2,1,0:T(8,128)(2,1)} %bitcast.2), calls=%async_computation | async-start | bytes 262144 | tf_op jit(solution)/shard_map/all_to_all | solution.py:8
  11.2 0.0 copy-start.1
  11.2 14.7 %all_gather.3 = bf16[512,128]{1,0:T(8,128)(2,1)S(1)} all-gather(bf16[128,128]{1,0:T(8,128)(2,1)S(1)} %broadcast_select_fusion), channel_id=1, replica_groups=mesh['sample'=2,'region'=4,'sub'=4] {'sub'}, dimensions={0}, use_global_device_ids=true | all-gather | bytes 163840 | tf_op jit(solution)/shard_map/all_gather | solution.py:24
  25.8 0.1 broadcast_in_dim.41
  25.9 0.1 broadcast_in_dim.42
  26.0 0.0 copy-done.1
  26.0 0.2 fusion.4
  26.2 0.0 copy-start.2
  26.2 0.0 all-to-all-done
  26.3 0.1 bitcast_select_fusion
  26.4 0.7 %copy-done.2 = bf16[128,512]{1,0:T(8,128)(2,1)S(1)} copy-done((bf16[128,512]{1,0:T(8,128)(2,1)S(1)}, bf16[128,512]{1,0:T(8,128)(2,1)}, u32[]{:S(2)}) %copy-start.2) | copy-done | bytes 131096
  27.1 0.2 fusion.2
  27.4 0.7 %copy.8 = f32[128,128]{1,0:T(8,128)} copy(f32[128,128]{0,1:T(8,128)S(1)} %fusion.2) | data formatting | bytes 131072 | tf_op jit(solution)/shard_map/jit(_where)/select_n | solution.py:37
  (1 shorter events, 0.0 us)
Async XLA Ops:
  0.0 2.8 %copy-start = (bf16[512,128]{1,0:T(8,128)(2,1)S(1)}, bf16[512,128]{1,0:T(8,128)(2,1)}, u32[]{:S(2)}) copy-start(bf16[512,128]{1,0:T(8,128)(2,1)} %param.9) | copy-start | bytes 393220
  0.0 0.7 %copy-start.3 = (s32[16]{0:T(128)S(1)}, s32[16]{0:T(128)}, u32[]{:S(2)}) copy-start(s32[16]{0:T(128)} %param.6) | copy-start | bytes 196
  3.8 22.5 %all-to-all-start = ((bf16[16,32,128]{2,1,0:T(8,128)(2,1)}), bf16[16,32,128]{2,1,0:T(8,128)(2,1)S(1)}, u32[]{:S(2)}, u32[]{:S(2)}) async-start(bf16[16,32,128]{2,1,0:T(8,128)(2,1)} %bitcast.2), calls=%async_computation | async-start | bytes 262144 | tf_op jit(solution)/shard_map/all_to_all | solution.py:8
  11.2 14.9 %copy-start.1 = (bf16[128,512]{1,0:T(8,128)(2,1)S(1)}, bf16[128,512]{1,0:T(8,128)(2,1)}, u32[]{:S(2)}) copy-start(bf16[128,512]{1,0:T(8,128)(2,1)} %param.7) | copy-start | bytes 393220
  26.2 0.9 %copy-start.2 = (bf16[128,512]{1,0:T(8,128)(2,1)S(1)}, bf16[128,512]{1,0:T(8,128)(2,1)}, u32[]{:S(2)}) copy-start(bf16[128,512]{1,0:T(8,128)(2,1)} %param.8) | copy-start | bytes 393220
where the time goes:
time: 28.4 us; the launch traced here: 28.1 us
  blocking collectives  14.7 us (52%)
  starting transfers between devices  7.39 us (26%)
  local copies, waits for them, and re-layouts  3.67 us (13%)
  other arithmetic  1.64 us (6%)
  matrix products  0.65 us (2%)
    all_gather x1, blocking collectives, local(): lax.all_gather(masked, 'sub', axis=0, tiled=True)  14.7 us
    all_to_all x1, starting transfers between devices, send_coefficients(): lax.all_to_all(coefficients, ('region', 'sub'), split_axis=0, concat_axis...  7.39 us
    unnamed x8, local copies, waits for them, and re-layouts  1.45 us
    select_n x1, other arithmetic, local(): masked = jnp.where(own_live, densities, jnp.zeros_like(densities))  0.84 us
    convert_element_type x1, local copies, waits for them, and re-layouts, local(): jnp.dot(column_factor, masked, preferred_element_type=jnp.float32)  0.75 us
    select_n x1, local copies, waits for them, and re-layouts, local(): return jnp.where(own_live, combined, jnp.zeros_like(combined))  0.73 us
    lt x1, other arithmetic, local(): own_live = slot_index < cluster_size[own_cluster]  0.65 us
    dynamic_slice x1, local copies, waits for them, and re-layouts, local(): own_live = slot_index < cluster_size[own_cluster]  0.58 us
  transfers between devices with their start and end apart: 1, of which 0 were waited for; matrix products, arithmetic and copies ran while one was open for 1% of the time, Pallas kernels for 0%

commit v1 on v0

--- a/solution.py
+++ b/solution.py
@@ -2,6 +2,22 @@
 import jax.numpy as jnp
 from jax import lax
 from jax.sharding import PartitionSpec as P
+
+
+def collect(x, axis, dim):
+    ways, here, hop = (lax.axis_size(axis), lax.axis_index(axis), x.shape[dim])
+    shape = [n * ways if d == dim else n for d, n in enumerate(x.shape)]
+    full = lax.dynamic_update_slice_in_dim(jnp.zeros(shape, x.dtype), x, here * hop, axis=dim)
+    going_up = going_down = x
+    for far in range(1, ways // 2 + 1):
+        going_up = lax.ppermute(going_up, axis, [(d, (d + 1) % ways) for d in range(ways)])
+        full = lax.dynamic_update_slice_in_dim(full, going_up, (here - far) % ways * hop, axis=dim)
+        if 2 * far < ways:
+            going_down = lax.ppermute(going_down, axis, [(d, (d - 1) % ways) for d in range(ways)])
+            full = lax.dynamic_update_slice_in_dim(
+                full, going_down, (here + far) % ways * hop, axis=dim
+            )
+    return full
 
 
 def send_coefficients(coefficients):
@@ -19,11 +35,7 @@
     slot_index = lax.broadcasted_iota(jnp.int32, (row_count, 1), 0)
     own_live = slot_index < cluster_size[own_cluster]
     masked = jnp.where(own_live, densities, jnp.zeros_like(densities))
-    near_sum = jnp.dot(
-        near_block,
-        lax.all_gather(masked, "sub", axis=0, tiled=True),
-        preferred_element_type=jnp.float32,
-    )
+    near_sum = jnp.dot(near_block, collect(masked, "sub", 0), preferred_element_type=jnp.float32)
     cluster_ids = jnp.arange(cluster_count, dtype=jnp.int32)
     far_flags = cluster_ids // group_count != region_id
     coefficients = jnp.dot(column_factor, masked, preferred_element_type=jnp.float32).astype(

time: 28.4 us -> 25.8 us (0.908)
  blocking collectives: 14.7 us -> 0 us
  starting transfers between devices: 7.39 us -> 13.2 us
  waiting for transfers between devices: 0.01 us -> 5.51 us
  local copies, waits for them, and re-layouts: 3.67 us -> 5.13 us
  other arithmetic: 1.64 us -> 0.89 us
    all_gather x1 -> x0, blocking collectives: 14.7 us -> none  [local(): lax.all_gather(masked, 'sub', axis=0, tiled=True)]
    ppermute x0 -> x3, starting transfers between devices: none -> 7.06 us  [the longest x1 5.13 us: collect(): lax.ppermute(going_down, axis, [(d, (d - 1) % ways) for d in range(ways)])]
    ppermute x0 -> x3, waiting for transfers between devices: none -> 5.51 us  [the longest x2 5.5 us: collect(): lax.ppermute(going_up, axis, [(d, (d + 1) % ways) for d in range(ways)])]
    unnamed x8 -> x10, local copies, waits for them, and re-layouts: 1.45 us -> 2.85 us
    all_to_all x1, starting transfers between devices: 7.39 us -> 6.13 us  [send_coefficients(): lax.all_to_all(coefficients, ('region', 'sub'), split_axis=0, concat_axis...]
    select_n x1 -> x0, other arithmetic: 0.84 us -> none  [local(): masked = jnp.where(own_live, densities, jnp.zeros_like(densities))]
  transfers between devices with their start and end apart: 1 -> 4, of which waited for: 0 -> 1; matrix products, arithmetic and copies ran while one was open for 1% -> 5% of each run, Pallas kernels for 0% -> 0%
where the time goes in v1:
time: 25.8 us; the launch traced here: 25.5 us
  starting transfers between devices  13.2 us (51%)
  waiting for transfers between devices  5.51 us (21%)
  local copies, waits for them, and re-layouts  5.13 us (20%)
  other arithmetic  0.89 us (3%)
  matrix products  0.65 us (3%)
    all_to_all x1, starting transfers between devices, send_coefficients(): lax.all_to_all(coefficients, ('region', 'sub'), split_axis=0, concat_axis...  6.13 us
    ppermute x2, waiting for transfers between devices, collect(): lax.ppermute(going_up, axis, [(d, (d + 1) % ways) for d in range(ways)])  5.5 us
    ppermute x1, starting transfers between devices, collect(): lax.ppermute(going_down, axis, [(d, (d - 1) % ways) for d in range(ways)])  5.13 us
    unnamed x10, local copies, waits for them, and re-layouts  2.85 us
    ppermute x2, starting transfers between devices, collect(): lax.ppermute(going_up, axis, [(d, (d + 1) % ways) for d in range(ways)])  1.93 us
    convert_element_type x1, local copies, waits for them, and re-layouts, local(): jnp.dot(column_factor, masked, preferred_element_type=jnp.float32)  0.75 us
    select_n x1, local copies, waits for them, and re-layouts, local(): return jnp.where(own_live, combined, jnp.zeros_like(combined))  0.73 us
    lt x1, other arithmetic, local(): own_live = slot_index < cluster_size[own_cluster]  0.65 us
  transfers between devices with their start and end apart: 4, of which 1 were waited for; matrix products, arithmetic and copies ran while one was open for 5% of the time, Pallas kernels for 0%

profile of v1, /device:TPU:0, one launch (start us, length us, event | category | flops | bytes accessed | tf_op | source)
XLA Modules:
  0.0 25.5 jit_solution(13145799297912497453)
XLA Ops:
  0.0 0.0 copy-start
  0.0 0.0 copy-start.4
  0.0 0.7 %copy-done.4 = s32[16]{0:T(128)S(1)} copy-done((s32[16]{0:T(128)S(1)}, s32[16]{0:T(128)}, u32[]{:S(2)}) %copy-start.4) | copy-done | bytes 88
  0.7 0.6 %dynamic_slice.3 = s32[1]{0:T(128)} dynamic-slice(s32[16]{0:T(128)S(1)} %copy-done.4, s32[]{:T(128)S(6)} %select_n.50), dynamic_slice_sizes={1} | dynamic-slice | bytes 12 | tf_op jit(solution)/shard_map/dynamic_slice | solution.py:36
  1.3 0.6 %iota_compare_fusion = pred[128]{0:T(512)(128)(4,1)S(1)} fusion(s32[]{:T(128)} %bitcast), kind=kLoop, calls=%fused_computation.16 | loop fusion | flops 128 | bytes 132 | tf_op jit(solution)/shard_map/lt | solution.py:36
  1.9 0.0 copy-start.3
  2.0 0.7 %copy-done.3 = bf16[128,128]{1,0:T(8,128)(2,1)S(1)} copy-done((bf16[128,128]{1,0:T(8,128)(2,1)S(1)}, bf16[128,128]{1,0:T(8,128)(2,1)}, u32[]{:S(2)}) %copy-start.3) | copy-done | bytes 32792
  2.7 0.1 constant_dynamic-update-slice_fusion.3
  2.8 5.1 %collective-permute-start.1 = (bf16[128,128]{1,0:T(8,128)(2,1)S(1)}, bf16[128,128]{1,0:T(8,128)(2,1)S(1)}, u32[]{:S(2)}, u32[]{:S(2)}) collective-permute-start(bf16[128,128]{1,0:T(8,128)(2,1)S(1)} %get-tuple-element.6), channel_id=1, source_target_pairs={{0,3},{1,0},{2,1},{3,2},{4,7},{5,4},{6,5},{7,6},{8,11},{9,8},{10,9... | collective-permute-start | bytes 98312 | tf_op jit(solution)/shard_map/ppermute | solution.py:16
  7.9 0.0 collective-permute-start
  7.9 0.0 copy-done
  7.9 0.2 fusion
  8.1 0.7 %copy.8 = bf16[512,128]{1,0:T(8,128)(2,1)} copy(bf16[512,128]{0,1:T(8,128)(2,1)S(1)} %fusion) | data formatting | bytes 262144 | tf_op jit(solution)/shard_map/convert_element_type | solution.py:41
  8.9 6.1 %all-to-all-start = ((bf16[16,32,128]{2,1,0:T(8,128)(2,1)}), bf16[16,32,128]{2,1,0:T(8,128)(2,1)S(1)}, u32[]{:S(2)}, u32[]{:S(2)}) async-start(bf16[16,32,128]{2,1,0:T(8,128)(2,1)} %bitcast.2), calls=%async_computation | async-start | bytes 262144 | tf_op jit(solution)/shard_map/all_to_all | solution.py:24
  15.1 0.1 broadcast_in_dim.38
  15.2 0.1 broadcast_in_dim.39
  15.3 0.0 collective-permute-done
  15.3 1.9 %collective-permute-start.2 = (bf16[128,128]{1,0:T(8,128)(2,1)S(1)}, bf16[128,128]{1,0:T(8,128)(2,1)S(1)}, u32[]{:S(2)}, u32[]{:S(2)}) collective-permute-start(bf16[128,128]{1,0:T(8,128)(2,1)S(1)} %collective-permute-done), channel_id=1, source_target_pairs={{0,1},{1,2},{2,3},{3,0},{4,5},{5,6},{6,7},{7,4},{8,9},{9,10},{10,1... | collective-permute-start | bytes 98312 | tf_op jit(solution)/shard_map/ppermute | solution.py:13
  17.2 0.0 collective-permute-done.1
  17.2 5.5 %collective-permute-done.2 = bf16[128,128]{1,0:T(8,128)(2,1)S(1)} collective-permute-done((bf16[128,128]{1,0:T(8,128)(2,1)S(1)}, bf16[128,128]{1,0:T(8,128)(2,1)S(1)}, u32[]{:S(2)}, u32[]{:S(2)}) %collective-permute-start.2) | collective-permute-done | bytes 32800 | tf_op jit(solution)/shard_map/ppermute | solution.py:13
  22.7 0.0 copy-start.1
  22.7 0.0 all-to-all-done
  22.8 0.1 bitcast_select_fusion
  22.9 0.7 %copy-done.1 = bf16[128,512]{1,0:T(8,128)(2,1)S(1)} copy-done((bf16[128,512]{1,0:T(8,128)(2,1)S(1)}, bf16[128,512]{1,0:T(8,128)(2,1)}, u32[]{:S(2)}) %copy-start.1) | copy-done | bytes 131096
  23.6 0.0 copy-start.2
  23.6 0.2 fusion.4
  23.9 0.7 %copy-done.2 = bf16[128,512]{1,0:T(8,128)(2,1)S(1)} copy-done((bf16[128,512]{1,0:T(8,128)(2,1)S(1)}, bf16[128,512]{1,0:T(8,128)(2,1)}, u32[]{:S(2)}) %copy-start.2) | copy-done | bytes 131096
  24.5 0.2 fusion.2
  24.8 0.7 %copy.9 = f32[128,128]{1,0:T(8,128)} copy(f32[128,128]{0,1:T(8,128)S(1)} %fusion.2) | data formatting | bytes 131072 | tf_op jit(solution)/shard_map/jit(_where)/select_n | solution.py:49
  (5 shorter events, 0.1 us)
Async XLA Ops:
  0.0 7.9 %copy-start = (bf16[512,128]{1,0:T(8,128)(2,1)S(1)}, bf16[512,128]{1,0:T(8,128)(2,1)}, u32[]{:S(2)}) copy-start(bf16[512,128]{1,0:T(8,128)(2,1)} %param.9) | copy-start | bytes 393220
  0.0 0.7 %copy-start.4 = (s32[16]{0:T(128)S(1)}, s32[16]{0:T(128)}, u32[]{:S(2)}) copy-start(s32[16]{0:T(128)} %param.6) | copy-start | bytes 196
  1.9 0.8 %copy-start.3 = (bf16[128,128]{1,0:T(8,128)(2,1)S(1)}, bf16[128,128]{1,0:T(8,128)(2,1)}, u32[]{:S(2)}) copy-start(bf16[128,128]{1,0:T(8,128)(2,1)} %param.5) | copy-start | bytes 98308
  2.8 14.4 %collective-permute-start.1 = (bf16[128,128]{1,0:T(8,128)(2,1)S(1)}, bf16[128,128]{1,0:T(8,128)(2,1)S(1)}, u32[]{:S(2)}, u32[]{:S(2)}) collective-permute-start(bf16[128,128]{1,0:T(8,128)(2,1)S(1)} %get-tuple-element.6), channel_id=1, source_target_pairs={{0,3},{1,0},{2,1},{3,2},{4,7},{5,4},{6,5},{7,6},{8,11},{9,8},{10,9... | collective-permute-start | bytes 98312 | tf_op jit(solution)/shard_map/ppermute | solution.py:16
  7.9 7.3 %collective-permute-start = (bf16[128,128]{1,0:T(8,128)(2,1)S(1)}, bf16[128,128]{1,0:T(8,128)(2,1)S(1)}, u32[]{:S(2)}, u32[]{:S(2)}) collective-permute-start(bf16[128,128]{1,0:T(8,128)(2,1)S(1)} %get-tuple-element.6), channel_id=1, source_target_pairs={{0,1},{1,2},{2,3},{3,0},{4,5},{5,6},{6,7},{7,4},{8,9},{9,10},{10,1... | collective-permute-start | bytes 98312 | tf_op jit(solution)/shard_map/ppermute | solution.py:13
  8.9 13.9 %all-to-all-start = ((bf16[16,32,128]{2,1,0:T(8,128)(2,1)}), bf16[16,32,128]{2,1,0:T(8,128)(2,1)S(1)}, u32[]{:S(2)}, u32[]{:S(2)}) async-start(bf16[16,32,128]{2,1,0:T(8,128)(2,1)} %bitcast.2), calls=%async_computation | async-start | bytes 262144 | tf_op jit(solution)/shard_map/all_to_all | solution.py:24
  15.3 7.5 %collective-permute-start.2 = (bf16[128,128]{1,0:T(8,128)(2,1)S(1)}, bf16[128,128]{1,0:T(8,128)(2,1)S(1)}, u32[]{:S(2)}, u32[]{:S(2)}) collective-permute-start(bf16[128,128]{1,0:T(8,128)(2,1)S(1)} %collective-permute-done), channel_id=1, source_target_pairs={{0,1},{1,2},{2,3},{3,0},{4,5},{5,6},{6,7},{7,4},{8,9},{9,10},{10,1... | collective-permute-start | bytes 98312 | tf_op jit(solution)/shard_map/ppermute | solution.py:13
  22.7 0.9 %copy-start.1 = (bf16[128,512]{1,0:T(8,128)(2,1)S(1)}, bf16[128,512]{1,0:T(8,128)(2,1)}, u32[]{:S(2)}) copy-start(bf16[128,512]{1,0:T(8,128)(2,1)} %param.8) | copy-start | bytes 393220
  23.6 0.9 %copy-start.2 = (bf16[128,512]{1,0:T(8,128)(2,1)S(1)}, bf16[128,512]{1,0:T(8,128)(2,1)}, u32[]{:S(2)}) copy-start(bf16[128,512]{1,0:T(8,128)(2,1)} %param.7) | copy-start | bytes 393220
